TPU v7x, 256 devices: a whole 4x4x8 slice. The times are simulated.
256 devices in a mesh: ctx: 8 (over x, core), tp: 32 (over y, z).
Axes of the slice: x: 4, y: 4, z: 8, core: 2. Of those that a mesh axis runs over, the one named last changes fastest.
Arguments:
- tokens: bfloat16 [1024, 8192], P('ctx', 'tp'), may hold values from -6 to 6
- in_weight: bfloat16 [8192, 3, 8192], P(None, None, 'tp'), may hold values from -0.0625 to 0.0625
- filter_taps: float32 [3, 3, 8192], P(None, None, 'tp'), may hold values from -2.4 to 2.4
- decay_rate: float32 [16, 8192], P(None, 'tp'), may hold values from 0.0001953125 to 0.08, as said below
- residue: float32 [16, 8192], P(None, 'tp'), may hold values from -80 to 80
Outputs:
- gated: bfloat16 [1024, 8192], P('ctx', 'tp')
Inputs may be any that keep to these rules, and one draw needn't show every extreme that they name: `decay_rate`: every decay rate lies between 0.2 / 1024 and 0.08.
All inputs are finite; a program needn't handle non-finite values.
Results may differ from a plain program's by a relative error of at most 0.015.
Values may be sent and summed in bfloat16 or wider, within the bound.
A program may use at most 128 MiB of HBM per device.

v0:
```python
import jax
import jax.numpy as jnp
from jax import lax
from jax.sharding import PartitionSpec as P

BLOCK = 128


def passed_along(value, axis, steps):
    count = lax.axis_size(axis)
    first, last = (max(0, -steps), min(count, count - steps))
    return lax.ppermute(value, axis, [(source, source + steps) for source in range(first, last)])


def entering(value, axis, join, neutral):
    count, mine = (lax.axis_size(axis), lax.axis_index(axis))
    pieces = jax.tree.map(lambda part: lax.all_gather(part, axis), value)
    total = jax.tree.map(
        lambda part, zero: jnp.full_like(part, 0) + jnp.asarray(zero, part.dtype), value, neutral
    )

    def step(position, total):
        longer = join(total, jax.tree.map(lambda part: part[position], pieces))
        return jax.tree.map(lambda new, old: jnp.where(position < mine, new, old), longer, total)

    return lax.fori_loop(0, count - 1, step, total)


def project(row_block, in_weight):
    weight_flat = in_weight.reshape(in_weight.shape[0], -1)
    gathered = lax.all_gather(row_block, "tp", axis=1, tiled=True)
    summed = jnp.dot(gathered, weight_flat, preferred_element_type=jnp.float32)
    return summed.astype(jnp.bfloat16).reshape(row_block.shape[0], 3, -1)


def combine_modes(earlier, later):
    return (earlier[0] * later[0], later[0] * earlier[1] + later[1])


def on_device(tokens, in_weight, filter_taps, decay_rate, residue):
    row_count = tokens.shape[0]
    lead_rows = filter_taps.shape[0] - 1
    projected = project(tokens, in_weight)
    rim_rows = passed_along(projected[row_count - lead_rows :], "ctx", 1)
    padded = jnp.concatenate([rim_rows, projected], axis=0)
    features = jnp.zeros((row_count,) + padded.shape[1:], jnp.float32)
    for lag_index in range(lead_rows + 1):
        window = padded[lead_rows - lag_index : lead_rows - lag_index + row_count].astype(
            jnp.float32
        )
        features = features + filter_taps[lag_index] * window
    query_part = features[:, 0]
    source = features[:, 1] * features[:, 2]
    chan_count = source.shape[1]
    block_count = row_count // BLOCK
    coeffs = residue * jnp.sqrt(1.0 - jnp.exp(-2.0 * decay_rate))
    offsets = jnp.arange(BLOCK, dtype=jnp.float32)
    falling = jnp.exp(-decay_rate[None] * offsets[:, None, None])
    rising = jnp.exp(decay_rate[None] * offsets[:, None, None])
    toeplitz = jnp.einsum(
        "inc,jnc->ijc", falling * coeffs[None], rising, precision=lax.Precision.HIGHEST
    )
    lower_mask = (offsets[:, None] >= offsets[None, :])[:, :, None]
    toeplitz = jnp.where(lower_mask, toeplitz, 0.0)
    blocks = source.reshape(block_count, BLOCK, chan_count)
    inner_part = jnp.einsum("ijc,bjc->bic", toeplitz, blocks, precision=lax.Precision.HIGHEST)
    end_weights = falling[::-1]
    partial_states = jnp.einsum(
        "jnc,bjc->bnc", end_weights, blocks, precision=lax.Precision.HIGHEST
    )
    block_decay = jnp.exp(-decay_rate * BLOCK)

    def advance(carry_state, block_term):
        return (block_decay * carry_state + block_term, carry_state)

    local_end, local_starts = lax.scan(advance, jnp.zeros_like(block_decay), partial_states)
    device_decay = jnp.exp(-decay_rate * row_count)
    identity = (jnp.ones_like(local_end), jnp.zeros_like(local_end))
    prefix = entering((device_decay, local_end), "ctx", combine_modes, identity)
    incoming = prefix[1]
    start_offsets = jnp.arange(block_count, dtype=jnp.float32) * BLOCK
    start_states = (
        local_starts + jnp.exp(-decay_rate[None] * start_offsets[:, None, None]) * incoming[None]
    )
    read_weights = coeffs[None] * jnp.exp(-decay_rate[None] * (offsets + 1.0)[:, None, None])
    carried = jnp.einsum(
        "inc,bnc->bic", read_weights, start_states, precision=lax.Precision.HIGHEST
    )
    response = (inner_part + carried).reshape(row_count, chan_count)
    return (query_part * response).astype(jnp.bfloat16)


def solution(mesh):
    return jax.shard_map(
        on_device,
        mesh=mesh,
        in_specs=(
            P("ctx", "tp"),
            P(None, None, "tp"),
            P(None, None, "tp"),
            P(None, "tp"),
            P(None, "tp"),
        ),
        out_specs=P("ctx", "tp"),
        check_vma=False,
    )
```

profile of v0, /device:TPU:5, one launch (start us, length us, event | category | flops | bytes accessed | tf_op | source)
XLA Modules:
  0.0 240.0 jit_solution(11823663511975442552)
XLA Ops:
  6.5 0.7 all-gather.4.cloned.1.call-update
  7.3 16.7 %copy.9 = bf16[8192,3,256]{0,2,1:T(8,128)(2,1)} copy(bf16[8192,3,256]{2,0,1:T(8,128)(2,1)} %param.8) | data formatting | bytes 25165824 | tf_op args[1]
  24.0 1.6 multiply_exponential_fusion.1
  25.6 1.6 multiply_exponential_fusion
  27.2 57.2 %all-gather.4.cloned.1.call-done = bf16[128,8192]{1,0:T(8,128)(2,1)} async-done(((bf16[128,256]{1,0:T(8,128)(2,1)}), bf16[128,8192]{1,0:T(8,128)(2,1)}) %all-gather.4.cloned.1.call-update) | async-done | bytes 2097168 | tf_op jit(solution)/shard_map/all_gather | solution.py:31
  84.5 9.5 %convolution_convert_fusion = bf16[128,768]{1,0:T(8,128)(2,1)S(1)} fusion(bf16[128,8192]{1,0:T(8,128)(2,1)} %all-gather.4.cloned.1.call-done, bf16[8192,768]{0,1:T(8,128)(2,1)} %bitcast.64), kind=kOutput, calls=%fused_computation.8 | convolution fusion | flops 1610711040 | bytes 14876672 | tf_op jit(solution)/shard_map/dot_general | solution.py:32
  94.0 0.2 copy.32
  94.2 6.3 %collective-permute-start = (bf16[2,3,256]{0,2,1:T(8,128)(2,1)S(1)}, bf16[2,3,256]{0,2,1:T(8,128)(2,1)S(1)}, u32[]{:S(2)}, u32[]{:S(2)}) collective-permute-start(bf16[2,3,256]{0,2,1:T(8,128)(2,1)S(1)} %bitcast.70), channel_id=1, source_target_pairs={{0,32},{32,64},{64,96},{96,128},{128,160},{160,192},{192,224},{1,3... | collective-permute-start | bytes 9224 | tf_op jit(solution)/shard_map/ppermute | solution.py:12
  100.6 2.5 %copy.13 = f32[128,16,256]{0,1,2:T(8,128)S(1)} copy(f32[128,16,256]{2,1,0:T(8,128)} %multiply_exponential_fusion.1) | data formatting | bytes 4194304 | tf_op jit(solution)/shard_map/exp | solution.py:59
  103.1 0.2 copy.10
  103.3 0.5 multiply_add_fusion
  104.0 1.8 multiply_reduce_fusion.1
  105.8 12.9 %all-gather = f32[128,256]{1,0:T(8,128)S(1)} all-gather(f32[16,256]{1,0:T(8,128)S(1)} %get-tuple-element.146), channel_id=2, replica_groups=mesh['ctx'=8,'tp'=32] {'ctx'}, dimensions={0}, use_global_device_ids=true | all-gather | bytes 147456 | tf_op jit(solution)/shard_map/all_gather | solution.py:17
  118.7 12.9 %all-gather.1 = f32[128,256]{1,0:T(8,128)S(1)} all-gather(f32[16,256]{1,0:T(8,128)S(1)} %get-tuple-element.145), channel_id=3, replica_groups=mesh['ctx'=8,'tp'=32] {'ctx'}, dimensions={0}, use_global_device_ids=true | all-gather | bytes 147456 | tf_op jit(solution)/shard_map/all_gather | solution.py:17
  131.7 0.3 while.9
  132.0 1.6 broadcast_multiply_fusion
  133.6 0.7 multiply_reduce_fusion
  134.4 3.4 %copy.14 = f32[128,16,256]{0,1,2:T(8,128)} copy(f32[128,16,256]{2,1,0:T(8,128)} %broadcast_multiply_fusion) | data formatting | bytes 4194304 | tf_op jit(solution)/shard_map/mul | solution.py:61
  137.7 29.8 %fusion.4 = f32[256,128,128]{2,1,0:T(8,128)} fusion(f32[128,16,256]{0,1,2:T(8,128)S(1)} %copy.13, f32[128,16,256]{0,1,2:T(8,128)} %copy.14), kind=kOutput, calls=%fused_computation.28 | convolution fusion | flops 805306368 | bytes 20971520 | tf_op jit(solution)/shard_map/inc,jnc->ijc/dot_general | solution.py:60
  167.5 17.8 %copy.15 = f32[256,128,128]{0,1,2:T(8,128)} copy(f32[256,128,128]{2,1,0:T(8,128)} %fusion.4) | data formatting | bytes 33554432 | tf_op jit(solution)/shard_map/inc,jnc->ijc/dot_general | solution.py:60
  185.3 12.2 %bitcast_select_fusion = f32[128,128,256]{2,1,0:T(8,128)} fusion(f32[256,128,128]{0,1,2:T(8,128)} %copy.15, pred[128,128]{1,0:T(8,128)(4,1)S(1)} %iota_compare_fusion), kind=kLoop, calls=%fused_computation.3 | loop fusion | flops 4194304 | bytes 33570816 | tf_op jit(solution)/shard_map/jit(_where)/select_n | solution.py:64
  197.5 18.3 %copy.17 = f32[128,128,256]{0,1,2:T(8,128)} copy(f32[128,128,256]{2,1,0:T(8,128)} %bitcast_select_fusion) | data formatting | bytes 33554432 | tf_op jit(solution)/shard_map/jit(_where)/select_n | solution.py:64
  215.8 16.6 %fusion.5 = f32[256,1,128]{2,1,0:T(1,128)S(1)} fusion(f32[128,256,1]{0,2,1:T(1,128)S(1)} %bitcast.66, f32[128,128,256]{0,1,2:T(8,128)} %copy.17), kind=kOutput, calls=%fused_computation.29 | convolution fusion | flops 50331648 | bytes 17039360 | tf_op jit(solution)/shard_map/ijc,bjc->bic/dot_general | solution.py:66
  232.4 0.7 copy.12
  (28 shorter events, 0.4 us)
Async XLA Ops:
  6.5 78.0 %all-gather.4.cloned.1.call-start = ((), (), s32[]{:S(2)}) async-start(), calls=%async_computation | async-start | bytes 2162688 | tf_op jit(solution)/shard_map/all_gather | solution.py:31
  7.3 16.7 %copy-start = (f32[16,256]{1,0:T(8,128)S(1)}, f32[16,256]{1,0:T(8,128)}, u32[]{:S(2)}) copy-start(f32[16,256]{1,0:T(8,128)} %param.10) | copy-start | bytes 49156
  7.3 16.7 %copy-start.2 = (f32[3,3,256]{2,1,0:T(4,128)S(1)}, f32[3,3,256]{2,1,0:T(4,128)}, u32[]{:S(2)}) copy-start(f32[3,3,256]{2,1,0:T(4,128)} %param.9) | copy-start | bytes 27652
  94.2 9.1 %collective-permute-start = (bf16[2,3,256]{0,2,1:T(8,128)(2,1)S(1)}, bf16[2,3,256]{0,2,1:T(8,128)(2,1)S(1)}, u32[]{:S(2)}, u32[]{:S(2)}) collective-permute-start(bf16[2,3,256]{0,2,1:T(8,128)(2,1)S(1)} %bitcast.70), channel_id=1, source_target_pairs={{0,32},{32,64},{64,96},{96,128},{128,160},{160,192},{192,224},{1,3... | collective-permute-start | bytes 9224 | tf_op jit(solution)/shard_map/ppermute | solution.py:12
  103.8 28.1 %copy-start.1 = (f32[16,256]{1,0:T(8,128)S(1)}, f32[16,256]{1,0:T(8,128)}, u32[]{:S(2)}) copy-start(f32[16,256]{1,0:T(8,128)} %param.11) | copy-start | bytes 49156
Sparse Core Ops, SparseCore 0:
  9.8 74.6 all-gather.3
where the time goes:
time: 243 us; the launch traced here: 240 us
  local copies, waits for them, and re-layouts  60 us (25%)
  waiting for transfers between devices  58 us (24%)
  matrix products  55.8 us (23%)
  blocking collectives  25.8 us (11%)
  other arithmetic  20.3 us (8%)
  between operations  13.6 us (6%)
  starting transfers between devices  6.34 us (3%)
    all_gather x1, waiting for transfers between devices, project(): gathered = lax.all_gather(row_block, 'tp', axis=1, tiled=True)  57.2 us
    dot_general x1, matrix products, on_device(): jnp.einsum('inc,jnc->ijc', falling * coeffs[None], rising, precision=lax....  29.8 us
    all_gather x2, blocking collectives, entering(): pieces = jax.tree.map(lambda part: lax.all_gather(part, axis), value)  25.8 us
    select_n x1, local copies, waits for them, and re-layouts, on_device(): toeplitz = jnp.where(lower_mask, toeplitz, 0.0)  18.3 us
    dot_general x1, local copies, waits for them, and re-layouts, on_device(): jnp.einsum('inc,jnc->ijc', falling * coeffs[None], rising, precision=lax....  17.8 us
    unnamed x8, local copies, waits for them, and re-layouts  16.8 us
    dot_general x1, matrix products, on_device(): jnp.einsum('ijc,bjc->bic', toeplitz, blocks, precision=lax.Precision.HIGH...  16.6 us
    select_n x1, other arithmetic, on_device(): toeplitz = jnp.where(lower_mask, toeplitz, 0.0)  12.2 us
  transfers between devices with their start and end apart: 2, of which 1 were waited for; matrix products, arithmetic and copies ran while one was open for 9% of the time, Pallas kernels for 0%

commit v1 on v0

v1 whole, which is shorter than its diff:
```python
import jax
import jax.numpy as jnp
from jax import lax
from jax.experimental import pallas as pl
from jax.experimental.pallas import tpu as pltpu
from jax.sharding import PartitionSpec as P

MESH = pl.DeviceIdType.MESH
PIECES = 2
LATENCY = 1.5
LEAD = 1.0
AHEAD = 12
LANES = 256
ROWS = 128
MODES = 16
HALO = 8


def torus(tp):
    return (4, 8) if tp == 32 else (2, tp // 2)


def plan(sizes, pieces):
    wide, deep = sizes
    steps = ((1, 0), (-1, 0), (0, 1), (0, -1))

    def far(v):
        return min(v[0], wide - v[0]) + min(v[1], deep - v[1])

    arrival = [{(0, 0): 0.0} for _ in range(pieces)]
    free = [0.0] * 4
    sends = []
    while len(sends) < pieces * (wide * deep - 1):
        choices = []
        for d, (dy, dz) in enumerate(steps):
            for h in range(pieces):
                for v, at in arrival[h].items():
                    w = ((v[0] + dy) % wide, (v[1] + dz) % deep)
                    if w not in arrival[h]:
                        start = max(at, free[d])
                        side = (h + d) % 2
                        choices.append((start, -far(w), side, h, d, v, w))
        start, _, _, h, d, v, w = min(choices)
        free[d] = start + 1.0
        arrival[h][w] = start + 1.0 + LATENCY
        sends.append((start, d, h, v, w))
    return sends, arrival


def body(sizes, tokens, weight, taps_hbm, decay_hbm, residue_hbm, out, buf, wbuf, acc, taps, decay, residue,
         reversed_fall, read, kern, kern_rows, proj, source, shifted, inner, query, pay, inbox,
         local_sem, weight_sem, send_sem, recv_sem, pay_send, pay_recv):
    wide, deep = sizes
    count = wide * deep
    ctx = lax.axis_size("ctx")
    me = lax.axis_index("tp")
    c = lax.axis_index("ctx")
    my, mz = me // deep, lax.rem(me, deep)
    sends, arrival = plan(sizes, PIECES)
    piece = ROWS // PIECES

    neighbours = (
        lax.rem(my + 1, wide) * deep + mz,
        lax.rem(my + wide - 1, wide) * deep + mz,
        my * deep + lax.rem(mz + 1, deep),
        my * deep + lax.rem(mz + deep - 1, deep),
    )

    def slot(v):
        return v[0] * deep + v[1]

    ready = sorted(
        ((max(arrival[h][v] for h in range(PIECES)), slot(v), v) for v in arrival[0]),
    )
    blocks = [v for _, _, v in ready]

    def weight_copy(v):
        owner = lax.rem(my - v[0] + wide, wide) * deep + lax.rem(mz - v[1] + deep, deep)
        rows = pl.ds(pl.multiple_of(owner * LANES, LANES), LANES)
        return pltpu.make_async_copy(weight.at[:, rows, :], wbuf.at[slot(v)], weight_sem.at[slot(v)])

    own = pltpu.make_async_copy(tokens, buf.at[0], local_sem.at[0])
    small = [
        pltpu.make_async_copy(taps_hbm, taps, local_sem.at[1]),
        pltpu.make_async_copy(decay_hbm, decay, local_sem.at[2]),
        pltpu.make_async_copy(residue_hbm, residue, local_sem.at[3]),
    ]

    inbox[...] = jnp.zeros_like(inbox)
    barrier = pltpu.get_barrier_semaphore()
    for n in neighbours:
        pl.semaphore_signal(barrier, inc=1, device_id={"tp": n}, device_id_type=MESH)
    for d in range(1, ctx):
        @pl.when(c - d >= 0)
        def _(d=d):
            pl.semaphore_signal(barrier, inc=1, device_id={"ctx": c - d}, device_id_type=MESH)
    own.start()
    for copy in small:
        copy.start()
    for v in blocks[:AHEAD]:
        weight_copy(v).start()
    proj[:, 0:HALO, :] = jnp.zeros((3, HALO, LANES), jnp.float32)
    source[0:HALO, :] = jnp.zeros((HALO, LANES), jnp.float32)
    kern[...] = jnp.zeros_like(kern)
    pl.semaphore_wait(barrier, 4 + ctx - 1 - c)

    def piece_copy(index, d, h, v, w):
        rows = pl.ds(h * piece, piece)
        src = tokens.at[rows] if v == (0, 0) else buf.at[slot(v), rows]
        return pltpu.make_async_remote_copy(
            src_ref=src,
            dst_ref=buf.at[slot(w), rows],
            send_sem=send_sem.at[index],
            recv_sem=recv_sem.at[h * count + slot(w)],
            device_id={"tp": neighbours[d]},
            device_id_type=MESH,
        )

    came = {}
    for index, (start, d, h, v, w) in enumerate(sends):
        came[(h, w)] = (index, d, h, v, w)
    arrived = {(h, (0, 0)) for h in range(PIECES)}

    def await_piece(h, v):
        if (h, v) not in arrived:
            arrived.add((h, v))
            piece_copy(*came[(h, v)]).wait_recv()

    def table(n):
        if n == 0:
            for copy in small:
                copy.wait()
        rate = decay[n : n + 1, :]
        coeff = residue[n : n + 1, :] * jnp.sqrt(1.0 - jnp.exp(-2.0 * rate))
        at = lax.broadcasted_iota(jnp.int32, (ROWS, LANES), 0).astype(jnp.float32)
        falling = jnp.exp(-rate * at)
        reversed_fall[n] = jnp.exp(-rate * (ROWS - 1.0 - at))
        read[n] = (coeff * jnp.exp(-rate)) * falling
        kern[HALO:, :] += coeff * falling

    def spread():
        @pl.loop(0, ROWS // 8)
        def _(q):
            rows = kern[pl.ds(pl.multiple_of(q * 8 + HALO, 8), 8), :]
            for r in range(8):
                kern_rows[r, q] = jnp.broadcast_to(rows[r : r + 1, :], (8, LANES))

    def multiply(order, v):
        if v == (0, 0):
            own.wait()
        for h in range(PIECES):
            await_piece(h, v)
        weight_copy(v).wait()
        lhs = buf[slot(v)]
        for s in range(3):
            part = jnp.dot(lhs, wbuf[slot(v), s], preferred_element_type=jnp.float32)
            if order == 0:
                acc[s] = part
            else:
                acc[s] += part

    events = [(max(arrival[s[2]][s[3]], s[0] - LEAD), 0, i) for i, s in enumerate(sends)]
    events += [(at, 1, i) for i, (at, _, _) in enumerate(ready)]
    tables = 0
    for at, kind, i in sorted(events):
        if kind == 0:
            start, d, h, v, w = sends[i]
            await_piece(h, v)
            piece_copy(i, d, h, v, w).start()
        else:
            if i + AHEAD < count:
                weight_copy(blocks[i + AHEAD]).start()
            multiply(i, blocks[i])
            if i < count - 1:
                for _ in range(-(-MODES * (i + 1) // (count - 4)) - tables):
                    if tables < MODES:
                        table(tables)
                        tables += 1
                        if tables == MODES:
                            spread()

    def features(s, first, rows):
        at = first + HALO
        total = taps[0, s : s + 1, :] * proj[s, at : at + rows, :]
        total = total + taps[1, s : s + 1, :] * proj[s, at - 1 : at - 1 + rows, :]
        return total + taps[2, s : s + 1, :] * proj[s, at - 2 : at - 2 + rows, :]

    for s in range(3):
        proj[s, HALO:, :] = acc[s].astype(jnp.bfloat16).astype(jnp.float32)
    rows_in = lax.broadcasted_iota(jnp.int32, (ROWS, LANES), 0)
    late = jnp.where(rows_in >= 2, features(1, 0, ROWS) * features(2, 0, ROWS), 0.0)
    source[HALO:, :] = late
    for n in range(MODES):
        pay[n : n + 1, :] = jnp.sum(reversed_fall[n] * late, axis=0, keepdims=True)
    end = HALO + ROWS
    pay[16:18, :] = proj[1, HALO : HALO + 2, :]
    pay[18:20, :] = proj[1, end - 2 : end, :]
    pay[20:22, :] = proj[2, HALO : HALO + 2, :]
    pay[22:24, :] = proj[2, end - 2 : end, :]
    pay[24:26, :] = proj[0, end - 2 : end, :]
    pay[26:32, :] = jnp.zeros((6, LANES), jnp.float32)

    def pay_copy(d):
        rows = pl.ds(0, 32 if d == 1 else 24)
        return pltpu.make_async_remote_copy(
            src_ref=pay.at[rows],
            dst_ref=inbox.at[d - 1, rows],
            send_sem=pay_send.at[d - 1],
            recv_sem=pay_recv.at[d - 1],
            device_id={"ctx": lax.rem(c + d, ctx)},
            device_id_type=MESH,
        )

    for d in range(1, ctx):
        @pl.when(c + d < ctx)
        def _(d=d):
            pay_copy(d).start()

    query[...] = features(0, 0, ROWS)
    for r in range(8):
        shifted[r] = source[HALO - r : HALO - r + ROWS, :]
    inner[...] = jnp.zeros_like(inner)

    @pl.loop(0, 8)
    def _(r):
        for half in range(LANES // 128):
            lanes = slice(half * 128, half * 128 + 128)
            late_rows = [shifted[r, 8 * i : 8 * i + 8, lanes] for i in range(ROWS // 8)]
            sums = [inner[8 * i : 8 * i + 8, lanes] for i in range(ROWS // 8)]
            for q in range(ROWS // 8):
                tap = kern_rows[r, q, :, lanes]
                for i in range(q, ROWS // 8):
                    sums[i] = sums[i] + tap * late_rows[i - q]
            for i in range(ROWS // 8):
                inner[8 * i : 8 * i + 8, lanes] = sums[i]

    rates = decay[...]
    over = jnp.exp(-rates * ROWS)
    from_first = jnp.exp(-rates * (ROWS - 1.0))
    from_second = jnp.exp(-rates * (ROWS - 2.0))

    for d in range(1, ctx):
        @pl.when(c - d >= 0)
        def _(d=d):
            pay_copy(d).wait_recv()

    def lead(d, s):
        base = 16 + 4 * (s - 1)
        first = inbox[d - 1, base : base + 1, :]
        second = inbox[d - 1, base + 1 : base + 2, :]
        if d < ctx - 1:
            before = inbox[d, base + 2 : base + 3, :]
            last = inbox[d, base + 3 : base + 4, :]
        else:
            before = last = jnp.zeros((1, LANES), jnp.float32)
        t0, t1, t2 = (taps[j, s : s + 1, :] for j in range(3))
        return t0 * first + t1 * last + t2 * before, t0 * second + t1 * first + t2 * last

    state = jnp.zeros((MODES, LANES), jnp.float32)
    for d in range(ctx - 1, 0, -1):
        key_first, key_second = lead(d, 1)
        value_first, value_second = lead(d, 2)
        left = inbox[d - 1, 0:MODES, :]
        left = left + from_first * (key_first * value_first) + from_second * (key_second * value_second)
        state = over * state + left

    proj[0, HALO - 2 : HALO, :] = inbox[0, 24:26, :]
    proj[1, HALO - 2 : HALO, :] = inbox[0, 18:20, :]
    proj[2, HALO - 2 : HALO, :] = inbox[0, 22:24, :]
    query[0:8, :] = features(0, 0, 8)
    early = features(1, 0, 8) * features(2, 0, 8)

    response = inner[...]
    response = response + kern[HALO:, :] * early[0:1, :] + kern[HALO - 1 : HALO - 1 + ROWS, :] * early[1:2, :]
    for n in range(MODES):
        response = response + read[n] * state[n : n + 1, :]
    out[...] = (query[...] * response).astype(out.dtype)

    for d in range(1, ctx):
        @pl.when(c + d < ctx)
        def _(d=d):
            pay_copy(d).wait_send()
    for i, (start, d, h, v, w) in enumerate(sends):
        piece_copy(i, d, h, v, w).wait_send()


def on_device(tokens, in_weight, filter_taps, decay_rate, residue):
    count = lax.axis_size("tp")
    ctx = lax.axis_size("ctx")
    sizes = torus(count)
    weight = jnp.transpose(in_weight, (1, 0, 2))
    hbm = pl.BlockSpec(memory_space=pltpu.MemorySpace.HBM)
    f32 = jnp.float32
    scratch = [
        pltpu.VMEM((count, ROWS, LANES), jnp.bfloat16),
        pltpu.VMEM((count, 3, LANES, LANES), jnp.bfloat16),
        pltpu.VMEM((3, ROWS, LANES), f32),
        pltpu.VMEM((3, 3, LANES), f32),
        pltpu.VMEM((MODES, LANES), f32),
        pltpu.VMEM((MODES, LANES), f32),
        pltpu.VMEM((MODES, ROWS, LANES), f32),
        pltpu.VMEM((MODES, ROWS, LANES), f32),
        pltpu.VMEM((HALO + ROWS, LANES), f32),
        pltpu.VMEM((8, ROWS // 8, 8, LANES), f32),
        pltpu.VMEM((3, HALO + ROWS, LANES), f32),
        pltpu.VMEM((HALO + ROWS, LANES), f32),
        pltpu.VMEM((8, ROWS, LANES), f32),
        pltpu.VMEM((ROWS, LANES), f32),
        pltpu.VMEM((ROWS, LANES), f32),
        pltpu.VMEM((32, LANES), f32),
        pltpu.VMEM((ctx - 1, 32, LANES), f32),
        pltpu.SemaphoreType.DMA((4,)),
        pltpu.SemaphoreType.DMA((count,)),
        pltpu.SemaphoreType.DMA((PIECES * (count - 1),)),
        pltpu.SemaphoreType.DMA((PIECES * count,)),
        pltpu.SemaphoreType.DMA((ctx - 1,)),
        pltpu.SemaphoreType.DMA((ctx - 1,)),
    ]

    def kernel(*refs):
        body(sizes, *refs)

    return pl.pallas_call(
        kernel,
        out_shape=jax.ShapeDtypeStruct((ROWS, LANES), jnp.bfloat16),
        in_specs=[hbm] * 5,
        out_specs=pl.BlockSpec(memory_space=pltpu.MemorySpace.VMEM),
        scratch_shapes=scratch,
        compiler_params=pltpu.CompilerParams(
            collective_id=0, has_side_effects=True, vmem_limit_bytes=56 * 1024 * 1024
        ),
        name="hyena",
    )(tokens, weight, filter_taps, decay_rate, residue)


def solution(mesh):
    return jax.shard_map(
        on_device,
        mesh=mesh,
        in_specs=(
            P("ctx", "tp"),
            P(None, None, "tp"),
            P(None, None, "tp"),
            P(None, "tp"),
            P(None, "tp"),
        ),
        out_specs=P("ctx", "tp"),
        check_vma=False,
    )
```

time: 243 us -> 37.4 us (0.15); the launches traced: 240 us -> 37.3 us
  local copies, waits for them, and re-layouts: 60 us -> 1.47 us
  waiting for transfers between devices: 58 us -> 0 us
  matrix products: 55.8 us -> 0 us
  Pallas kernels: 0 us -> 35.8 us
  blocking collectives: 25.8 us -> 0 us
  other arithmetic: 20.3 us -> 0 us
  between operations: 13.6 us -> 0.01 us
  starting transfers between devices: 6.34 us -> 0 us
    all_gather x1 -> x0, waiting for transfers between devices: 57.2 us -> none  [project(): gathered = lax.all_gather(row_block, 'tp', axis=1, tiled=True)]
    dot_general x3 -> x0, matrix products: 55.8 us -> none  [the longest x1 29.8 us: on_device(): jnp.einsum('inc,jnc->ijc', falling * coeffs[None], rising, precision=lax....]
    pallas_call x0 -> x1, Pallas kernels: none -> 35.8 us  [on_device(): pl.pallas_call(kernel, out_shape=jax.ShapeDtypeStruct((ROWS, LANES), jnp....]
    all_gather x2 -> x0, blocking collectives: 25.8 us -> none  [entering(): pieces = jax.tree.map(lambda part: lax.all_gather(part, axis), value)]
    select_n x1 -> x0, local copies, waits for them, and re-layouts: 18.3 us -> none  [on_device(): toeplitz = jnp.where(lower_mask, toeplitz, 0.0)]
    dot_general x2 -> x0, local copies, waits for them, and re-layouts: 17.9 us -> none  [the longest x1 17.8 us: on_device(): jnp.einsum('inc,jnc->ijc', falling * coeffs[None], rising, precision=lax....]
    unnamed x8 -> x1, local copies, waits for them, and re-layouts: 16.8 us -> 1.47 us
    select_n x8 -> x0, other arithmetic: 12.3 us -> none  [the longest x1 12.2 us: on_device(): toeplitz = jnp.where(lower_mask, toeplitz, 0.0)]
  transfers between devices with their start and end apart: 2 -> 0, of which waited for: 1 -> 0; matrix products, arithmetic and copies ran while one was open for 9% -> 0% of each run, Pallas kernels for 0% -> 0%
where the time goes in v1:
time: 37.4 us; the launch traced here: 37.3 us
  Pallas kernels  35.8 us (96%)
  local copies, waits for them, and re-layouts  1.47 us (4%)
    pallas_call x1, Pallas kernels, on_device(): pl.pallas_call(kernel, out_shape=jax.ShapeDtypeStruct((ROWS, LANES), jnp....  35.8 us
    unnamed x1, local copies, waits for them, and re-layouts  1.47 us

profile of v1, /device:TPU:5, one launch (start us, length us, event | category | flops | bytes accessed | tf_op | source)
XLA Modules:
  0.0 37.3 jit_solution(7835500334004011761)
XLA Ops:
  0.0 35.8 %hyena.1 = bf16[128,256]{1,0:T(8,128)(2,1)} custom-call(bf16[128,256]{1,0:T(8,128)(2,1)} %refs_0_.1, bf16[3,8192,256]{2,1,0:T(8,128)(2,1)} %bitcast.1, f32[3,3,256]{2,1,0:T(4,128)} %refs_2_.1, f32[16,256]{1,0:T(8,128)} %refs_3_.1, f32[16,256]{1,0:T(8,128)} %refs_4_.1), custom_call_target="tpu_custom_call" | custom-call | tf_op jit(solution)/shard_map/hyena/pallas_call | solution.py:323
  35.8 1.5 %copy.7 = bf16[128,256]{1,0:T(8,128)(2,1)} copy(bf16[128,256]{1,0:T(8,128)(2,1)} %hyena.1) | data formatting | bytes 131072

commit v2 on v1

--- a/solution.py
+++ b/solution.py
@@ -7,77 +7,62 @@
 
 MESH = pl.DeviceIdType.MESH
 PIECES = 2
-LATENCY = 1.5
-LEAD = 1.0
+PLAN = (
+    (1, 0, 0, 1, 0), (0, 0, 0, 0, -1), (0, 0, 0, 0, 1), (0, 0, 0, -1, 0), (0, 0), (1, 0, 0, -1, 0), (1, 0, 0, 0, 1),
+    (1, 0, 0, 0, -1), (0, 0, 0, 1, 0), (1, 0, 0, 0, -2), (0, 0, 0, 0, 2), (0, 3, 0, 0, -1), (0, 0, 1, -1, 0),
+    (0, 0, 7, 1, 0), (1, 1, 0, 0, 1), (0, 0, 7, 0, -1), (1, 0, 7, 1, 0), (1, 0, 7, -1, 0), (1, 3, 0, 0, 1), (0, 1),
+    (0, 7), (1, 0), (3, 0), (0, 1, 0, 0, 1), (0, 1, 0, 1, 0), (1, 3, 0, -1, 0), (1, 0, 6, 0, -1), (1, 0, 6, -1, 0),
+    (0, 0, 2, 0, 1), (1, 0, 6, 1, 0), (1, 0, 6, 0, -2), (0, 0, 2, 1, 0), (0, 0, 2, -1, 0), (1, 1, 1, 0, 1),
+    (1, 1, 1, 1, 0), (0, 3, 7, -1, 0), (1, 3, 1, 0, 1), (0, 0, 6, 0, -1), (1, 3, 7, -1, 0), (0, 0, 6, 1, 0), (0, 6),
+    (1, 7), (3, 1), (3, 7), (0, 3, 7, 0, -1), (0, 2, 0, 0, 1), (1, 1), (2, 0), (1, 0, 5, -1, 0), (1, 0, 5, 1, 0),
+    (0, 0, 3, 0, 1), (0, 0, 3, -1, 0), (1, 3, 6, 0, -2), (0, 0, 3, 1, 0), (0, 1, 2, 0, 2), (0, 3, 2, -1, 0),
+    (1, 1, 2, 1, 0), (1, 2), (1, 0, 4, 1, 0), (0, 2, 7, 0, -1), (1, 3, 2, 0, 1), (3, 2), (0, 0, 5, -1, 0), (0, 5),
+    (0, 0, 5, 1, 0), (1, 2, 7, 0, -1), (1, 6), (2, 7), (1, 1, 2, 0, 1), (1, 0, 4, 0, -1), (2, 1), (3, 6),
+    (1, 3, 2, 1, 0), (1, 3, 5, -1, 0), (0, 2, 7, 0, -2), (0, 4), (0, 3, 3, 0, 1), (0, 3, 3, -1, 0), (1, 3, 4, -1, 0),
+    (0, 1, 4, 1, 0), (1, 2, 2, 0, 1), (2, 2), (1, 4), (3, 5), (3, 3), (2, 6), (1, 5), (1, 3), (0, 3), (0, 2), (3, 4),
+    (2, 5), (2, 3), (2, 4),
+)
 AHEAD = 12
+FIRST_TABLE = 2
 LANES = 256
 ROWS = 128
 MODES = 16
 HALO = 8
 
 
-def torus(tp):
-    return (4, 8) if tp == 32 else (2, tp // 2)
-
-
-def plan(sizes, pieces):
-    wide, deep = sizes
-    steps = ((1, 0), (-1, 0), (0, 1), (0, -1))
-
-    def far(v):
-        return min(v[0], wide - v[0]) + min(v[1], deep - v[1])
-
-    arrival = [{(0, 0): 0.0} for _ in range(pieces)]
-    free = [0.0] * 4
-    sends = []
-    while len(sends) < pieces * (wide * deep - 1):
-        choices = []
-        for d, (dy, dz) in enumerate(steps):
-            for h in range(pieces):
-                for v, at in arrival[h].items():
-                    w = ((v[0] + dy) % wide, (v[1] + dz) % deep)
-                    if w not in arrival[h]:
-                        start = max(at, free[d])
-                        side = (h + d) % 2
-                        choices.append((start, -far(w), side, h, d, v, w))
-        start, _, _, h, d, v, w = min(choices)
-        free[d] = start + 1.0
-        arrival[h][w] = start + 1.0 + LATENCY
-        sends.append((start, d, h, v, w))
-    return sends, arrival
-
-
-def body(sizes, tokens, weight, taps_hbm, decay_hbm, residue_hbm, out, buf, wbuf, acc, taps, decay, residue,
+WIDE, DEEP = 4, 8
+GROUP = 4
+
+
+def body(tokens, weight, taps_hbm, decay_hbm, residue_hbm, out, buf, wbuf, acc, taps, decay, residue,
          reversed_fall, read, kern, kern_rows, proj, source, shifted, inner, query, pay, inbox,
          local_sem, weight_sem, send_sem, recv_sem, pay_send, pay_recv):
-    wide, deep = sizes
-    count = wide * deep
+    count = WIDE * DEEP
     ctx = lax.axis_size("ctx")
     me = lax.axis_index("tp")
     c = lax.axis_index("ctx")
-    my, mz = me // deep, lax.rem(me, deep)
-    sends, arrival = plan(sizes, PIECES)
+    my, mz = me // DEEP, lax.rem(me, DEEP)
+    sends = [p for p in PLAN if len(p) == 5]
+    blocks = [p for p in PLAN if len(p) == 2]
     piece = ROWS // PIECES
-
-    neighbours = (
-        lax.rem(my + 1, wide) * deep + mz,
-        lax.rem(my + wide - 1, wide) * deep + mz,
-        my * deep + lax.rem(mz + 1, deep),
-        my * deep + lax.rem(mz + deep - 1, deep),
-    )
+    turn = 1
+
+    def at_offset(dy, dz):
+        return lax.rem(my + turn * dy + 2 * WIDE, WIDE) * DEEP + lax.rem(mz + turn * dz + 2 * DEEP, DEEP)
+
+    steps = sorted({p[3:] for p in sends})
+    slots = {v: i for i, v in enumerate(blocks)}
 
     def slot(v):
-        return v[0] * deep + v[1]
-
-    ready = sorted(
-        ((max(arrival[h][v] for h in range(PIECES)), slot(v), v) for v in arrival[0]),
-    )
-    blocks = [v for _, _, v in ready]
+        return slots[v]
 
     def weight_copy(v):
-        owner = lax.rem(my - v[0] + wide, wide) * deep + lax.rem(mz - v[1] + deep, deep)
-        rows = pl.ds(pl.multiple_of(owner * LANES, LANES), LANES)
-        return pltpu.make_async_copy(weight.at[:, rows, :], wbuf.at[slot(v)], weight_sem.at[slot(v)])
+        rows = pl.ds(pl.multiple_of(at_offset(-v[0], -v[1]) * LANES, LANES), LANES)
+        return pltpu.make_async_copy(weight.at[:, rows, :], wbuf.at[slot(v)], weight_sem.at[slot(v) // GROUP])
+
+    def weight_wait(group):
+        some = wbuf.at[pl.ds(group * GROUP, GROUP)]
+        pltpu.make_async_copy(some, some, weight_sem.at[group]).wait()
 
     own = pltpu.make_async_copy(tokens, buf.at[0], local_sem.at[0])
     small = [
@@ -86,10 +71,10 @@
         pltpu.make_async_copy(residue_hbm, residue, local_sem.at[3]),
     ]
 
+    barrier = pltpu.get_barrier_semaphore()
+    for dy, dz in steps:
+        pl.semaphore_signal(barrier, inc=1, device_id={"tp": at_offset(-dy, -dz)}, device_id_type=MESH)
     inbox[...] = jnp.zeros_like(inbox)
-    barrier = pltpu.get_barrier_semaphore()
-    for n in neighbours:
-        pl.semaphore_signal(barrier, inc=1, device_id={"tp": n}, device_id_type=MESH)
     for d in range(1, ctx):
         @pl.when(c - d >= 0)
         def _(d=d):
@@ -102,29 +87,40 @@
     proj[:, 0:HALO, :] = jnp.zeros((3, HALO, LANES), jnp.float32)
     source[0:HALO, :] = jnp.zeros((HALO, LANES), jnp.float32)
     kern[...] = jnp.zeros_like(kern)
-    pl.semaphore_wait(barrier, 4 + ctx - 1 - c)
-
-    def piece_copy(index, d, h, v, w):
+    pl.semaphore_wait(barrier, len(steps) + ctx - 1 - c)
+
+    passed = {(h, (y, z)) for h, y, z, _, _ in sends}
+    kept = sorted(p for p in passed if p[1] != (0, 0))
+    order_of = {p: i for i, p in enumerate(kept)}
+    leaves = {v: [h for h in range(PIECES) if (h, v) not in passed] for v in blocks}
+
+    def recv_at(h, w):
+        return recv_sem.at[order_of[h, w] if (h, w) in passed else len(kept) + slot(w)]
+
+    def piece_copy(step, h, v, w):
         rows = pl.ds(h * piece, piece)
         src = tokens.at[rows] if v == (0, 0) else buf.at[slot(v), rows]
         return pltpu.make_async_remote_copy(
             src_ref=src,
             dst_ref=buf.at[slot(w), rows],
-            send_sem=send_sem.at[index],
-            recv_sem=recv_sem.at[h * count + slot(w)],
-            device_id={"tp": neighbours[d]},
+            send_sem=send_sem.at[0],
+            recv_sem=recv_at(h, w),
+            device_id={"tp": at_offset(*step)},
             device_id_type=MESH,
         )
 
-    came = {}
-    for index, (start, d, h, v, w) in enumerate(sends):
-        came[(h, w)] = (index, d, h, v, w)
     arrived = {(h, (0, 0)) for h in range(PIECES)}
 
     def await_piece(h, v):
         if (h, v) not in arrived:
             arrived.add((h, v))
-            piece_copy(*came[(h, v)]).wait_recv()
+            ref = buf.at[slot(v), pl.ds(h * piece, piece)]
+            pltpu.make_async_copy(ref, ref, recv_at(h, v)).wait()
+
+    def await_leaves(v):
+        if leaves[v]:
+            ref = buf.at[slot(v), pl.ds(0, piece * len(leaves[v]))]
+            pltpu.make_async_copy(ref, ref, recv_at(leaves[v][0], v)).wait()
 
     def table(n):
         if n == 0:
@@ -149,8 +145,11 @@
         if v == (0, 0):
             own.wait()
         for h in range(PIECES):
-            await_piece(h, v)
-        weight_copy(v).wait()
+            if (h, v) in passed:
+                await_piece(h, v)
+        await_leaves(v)
+        if order % GROUP == 0:
+            weight_wait(order // GROUP)
         lhs = buf[slot(v)]
         for s in range(3):
             part = jnp.dot(lhs, wbuf[slot(v), s], preferred_element_type=jnp.float32)
@@ -159,25 +158,23 @@
             else:
                 acc[s] += part
 
-    events = [(max(arrival[s[2]][s[3]], s[0] - LEAD), 0, i) for i, s in enumerate(sends)]
-    events += [(at, 1, i) for i, (at, _, _) in enumerate(ready)]
     tables = 0
-    for at, kind, i in sorted(events):
-        if kind == 0:
-            start, d, h, v, w = sends[i]
+    for p in PLAN:
+        if len(p) == 5:
+            h, v, step = p[0], p[1:3], p[3:]
+            w = (v[0] + step[0]) % WIDE, (v[1] + step[1]) % DEEP
             await_piece(h, v)
-            piece_copy(i, d, h, v, w).start()
-        else:
-            if i + AHEAD < count:
-                weight_copy(blocks[i + AHEAD]).start()
-            multiply(i, blocks[i])
-            if i < count - 1:
-                for _ in range(-(-MODES * (i + 1) // (count - 4)) - tables):
-                    if tables < MODES:
-                        table(tables)
-                        tables += 1
-                        if tables == MODES:
-                            spread()
+            piece_copy(step, h, v, w).start()
+            continue
+        i = slot(p)
+        if i + AHEAD < count:
+            weight_copy(blocks[i + AHEAD]).start()
+        multiply(i, p)
+        if tables < MODES and i >= FIRST_TABLE:
+            table(tables)
+            tables += 1
+            if tables == MODES:
+                spread()
 
     def features(s, first, rows):
         at = first + HALO
@@ -280,14 +277,19 @@
         @pl.when(c + d < ctx)
         def _(d=d):
             pay_copy(d).wait_send()
-    for i, (start, d, h, v, w) in enumerate(sends):
-        piece_copy(i, d, h, v, w).wait_send()
+    sent = buf.at[pl.ds(0, count - 1)]
+    pltpu.make_async_copy(sent, sent, send_sem.at[0]).wait()
+
+
+def recv_count():
+    passed = {p[:3] for p in PLAN if len(p) == 5 and p[1:3] != (0, 0)}
+    return len(passed) + WIDE * DEEP
 
 
 def on_device(tokens, in_weight, filter_taps, decay_rate, residue):
     count = lax.axis_size("tp")
     ctx = lax.axis_size("ctx")
-    sizes = torus(count)
+    assert count == WIDE * DEEP
     weight = jnp.transpose(in_weight, (1, 0, 2))
     hbm = pl.BlockSpec(memory_space=pltpu.MemorySpace.HBM)
     f32 = jnp.float32
@@ -310,15 +312,15 @@
         pltpu.VMEM((32, LANES), f32),
         pltpu.VMEM((ctx - 1, 32, LANES), f32),
         pltpu.SemaphoreType.DMA((4,)),
-        pltpu.SemaphoreType.DMA((count,)),
-        pltpu.SemaphoreType.DMA((PIECES * (count - 1),)),
-        pltpu.SemaphoreType.DMA((PIECES * count,)),
+        pltpu.SemaphoreType.DMA((count // GROUP,)),
+        pltpu.SemaphoreType.DMA((1,)),
+        pltpu.SemaphoreType.DMA((recv_count(),)),
         pltpu.SemaphoreType.DMA((ctx - 1,)),
         pltpu.SemaphoreType.DMA((ctx - 1,)),
     ]
 
     def kernel(*refs):
-        body(sizes, *refs)
+        body(*refs)
 
     return pl.pallas_call(
         kernel,

time: 37.4 us -> 33.8 us (0.904)
  Pallas kernels: 35.8 us -> 32.2 us
    pallas_call x1, Pallas kernels: 35.8 us -> 32.2 us  [on_device(): pl.pallas_call(kernel, out_shape=jax.ShapeDtypeStruct((ROWS, LANES), jnp....]
where the time goes in v2:
time: 33.8 us; the launch traced here: 33.7 us
  Pallas kernels  32.2 us (95%)
  local copies, waits for them, and re-layouts  1.47 us (4%)
    pallas_call x1, Pallas kernels, on_device(): pl.pallas_call(kernel, out_shape=jax.ShapeDtypeStruct((ROWS, LANES), jnp....  32.2 us
    unnamed x1, local copies, waits for them, and re-layouts  1.47 us

profile of v2, /device:TPU:5, one launch (start us, length us, event | category | flops | bytes accessed | tf_op | source)
XLA Modules:
  0.0 33.7 jit_solution(2164565660358960682)
XLA Ops:
  0.0 32.2 %hyena.1 = bf16[128,256]{1,0:T(8,128)(2,1)} custom-call(bf16[128,256]{1,0:T(8,128)(2,1)} %refs_0_.1, bf16[3,8192,256]{2,1,0:T(8,128)(2,1)} %bitcast.1, f32[3,3,256]{2,1,0:T(4,128)} %refs_2_.1, f32[16,256]{1,0:T(8,128)} %refs_3_.1, f32[16,256]{1,0:T(8,128)} %refs_4_.1), custom_call_target="tpu_custom_call" | custom-call | tf_op jit(solution)/shard_map/hyena/pallas_call | solution.py:325
  32.2 1.5 %copy.7 = bf16[128,256]{1,0:T(8,128)(2,1)} copy(bf16[128,256]{1,0:T(8,128)(2,1)} %hyena.1) | data formatting | bytes 131072

commit v3 on v2

--- a/solution.py
+++ b/solution.py
@@ -35,7 +35,7 @@
 
 
 def body(tokens, weight, taps_hbm, decay_hbm, residue_hbm, out, buf, wbuf, acc, taps, decay, residue,
-         reversed_fall, read, kern, kern_rows, proj, source, shifted, inner, query, pay, inbox,
+         reversed_fall, read, kern, kern_rows, proj, source, shifted, inner, query, pay, inbox, rim, rim_in, query_rim, query_in,
          local_sem, weight_sem, send_sem, recv_sem, pay_send, pay_recv):
     count = WIDE * DEEP
     ctx = lax.axis_size("ctx")
@@ -75,6 +75,9 @@
     for dy, dz in steps:
         pl.semaphore_signal(barrier, inc=1, device_id={"tp": at_offset(-dy, -dz)}, device_id_type=MESH)
     inbox[...] = jnp.zeros_like(inbox)
+    rim_in[...] = jnp.zeros_like(rim_in)
+    query_in[...] = jnp.zeros_like(query_in)
+    query_rim[...] = jnp.zeros_like(query_rim)
     for d in range(1, ctx):
         @pl.when(c - d >= 0)
         def _(d=d):
@@ -182,36 +185,56 @@
         total = total + taps[1, s : s + 1, :] * proj[s, at - 1 : at - 1 + rows, :]
         return total + taps[2, s : s + 1, :] * proj[s, at - 2 : at - 2 + rows, :]
 
-    for s in range(3):
-        proj[s, HALO:, :] = acc[s].astype(jnp.bfloat16).astype(jnp.float32)
+    def project(s):
+        rounded = acc[s].astype(jnp.bfloat16)
+        proj[s, HALO:, :] = rounded.astype(jnp.float32)
+        return rounded
+
+    def copy_to(d, src, dst, index):
+        return pltpu.make_async_remote_copy(
+            src_ref=src,
+            dst_ref=dst,
+            send_sem=pay_send.at[index],
+            recv_sem=pay_recv.at[index],
+            device_id={"ctx": lax.rem(c + d, ctx)},
+            device_id_type=MESH,
+        )
+
+    def rim_copy(d):
+        return copy_to(d, rim, rim_in.at[d - 1], d - 1)
+
+    def pay_copy(d):
+        return copy_to(d, pay, inbox.at[d - 1], ctx - 1 + d - 1)
+
+    def query_copy():
+        return copy_to(1, query_rim, query_in, 2 * (ctx - 1))
+
+    def to_later(act):
+        for d in range(1, ctx):
+            @pl.when(c + d < ctx)
+            def _(d=d):
+                act(d)
+
+    def from_earlier(act):
+        for d in range(1, ctx):
+            @pl.when(c - d >= 0)
+            def _(d=d):
+                act(d)
+
+    key, value = project(1), project(2)
+    rim[...] = jnp.concatenate([key[0:2], key[ROWS - 2 :], value[0:2], value[ROWS - 2 :]], axis=0)
+    to_later(lambda d: rim_copy(d).start())
     rows_in = lax.broadcasted_iota(jnp.int32, (ROWS, LANES), 0)
     late = jnp.where(rows_in >= 2, features(1, 0, ROWS) * features(2, 0, ROWS), 0.0)
     source[HALO:, :] = late
     for n in range(MODES):
         pay[n : n + 1, :] = jnp.sum(reversed_fall[n] * late, axis=0, keepdims=True)
-    end = HALO + ROWS
-    pay[16:18, :] = proj[1, HALO : HALO + 2, :]
-    pay[18:20, :] = proj[1, end - 2 : end, :]
-    pay[20:22, :] = proj[2, HALO : HALO + 2, :]
-    pay[22:24, :] = proj[2, end - 2 : end, :]
-    pay[24:26, :] = proj[0, end - 2 : end, :]
-    pay[26:32, :] = jnp.zeros((6, LANES), jnp.float32)
-
-    def pay_copy(d):
-        rows = pl.ds(0, 32 if d == 1 else 24)
-        return pltpu.make_async_remote_copy(
-            src_ref=pay.at[rows],
-            dst_ref=inbox.at[d - 1, rows],
-            send_sem=pay_send.at[d - 1],
-            recv_sem=pay_recv.at[d - 1],
-            device_id={"ctx": lax.rem(c + d, ctx)},
-            device_id_type=MESH,
-        )
-
-    for d in range(1, ctx):
-        @pl.when(c + d < ctx)
-        def _(d=d):
-            pay_copy(d).start()
+    to_later(lambda d: pay_copy(d).start())
+    query_rim[0:2, :] = project(0)[ROWS - 2 :]
+
+    @pl.when(c + 1 < ctx)
+    def _():
+        query_copy().start()
 
     query[...] = features(0, 0, ROWS)
     for r in range(8):
@@ -236,18 +259,14 @@
     from_first = jnp.exp(-rates * (ROWS - 1.0))
     from_second = jnp.exp(-rates * (ROWS - 2.0))
 
-    for d in range(1, ctx):
-        @pl.when(c - d >= 0)
-        def _(d=d):
-            pay_copy(d).wait_recv()
+    from_earlier(lambda d: rim_copy(d).wait_recv())
+    rims = [rim_in[d].astype(jnp.float32) for d in range(ctx - 1)]
 
     def lead(d, s):
-        base = 16 + 4 * (s - 1)
-        first = inbox[d - 1, base : base + 1, :]
-        second = inbox[d - 1, base + 1 : base + 2, :]
+        base = 4 * (s - 1)
+        first, second = rims[d - 1][base : base + 1], rims[d - 1][base + 1 : base + 2]
         if d < ctx - 1:
-            before = inbox[d, base + 2 : base + 3, :]
-            last = inbox[d, base + 3 : base + 4, :]
+            before, last = rims[d][base + 2 : base + 3], rims[d][base + 3 : base + 4]
         else:
             before = last = jnp.zeros((1, LANES), jnp.float32)
         t0, t1, t2 = (taps[j, s : s + 1, :] for j in range(3))
@@ -257,26 +276,39 @@
     for d in range(ctx - 1, 0, -1):
         key_first, key_second = lead(d, 1)
         value_first, value_second = lead(d, 2)
-        left = inbox[d - 1, 0:MODES, :]
-        left = left + from_first * (key_first * value_first) + from_second * (key_second * value_second)
+        left = from_first * (key_first * value_first) + from_second * (key_second * value_second)
         state = over * state + left
 
-    proj[0, HALO - 2 : HALO, :] = inbox[0, 24:26, :]
-    proj[1, HALO - 2 : HALO, :] = inbox[0, 18:20, :]
-    proj[2, HALO - 2 : HALO, :] = inbox[0, 22:24, :]
+    proj[1, HALO - 2 : HALO, :] = rims[0][2:4]
+    proj[2, HALO - 2 : HALO, :] = rims[0][6:8]
+    early = features(1, 0, 8) * features(2, 0, 8)
+    inner[...] += kern[HALO:, :] * early[0:1, :] + kern[HALO - 1 : HALO - 1 + ROWS, :] * early[1:2, :]
+
+    @pl.when(c > 0)
+    def _():
+        query_copy().wait_recv()
+
+    proj[0, HALO - 2 : HALO, :] = query_in[0:2, :].astype(jnp.float32)
     query[0:8, :] = features(0, 0, 8)
-    early = features(1, 0, 8) * features(2, 0, 8)
+
+    from_earlier(lambda d: pay_copy(d).wait_recv())
+    others = jnp.zeros((MODES, LANES), jnp.float32)
+    for d in range(ctx - 1, 0, -1):
+        others = over * others + inbox[d - 1]
+    state = state + others
 
     response = inner[...]
-    response = response + kern[HALO:, :] * early[0:1, :] + kern[HALO - 1 : HALO - 1 + ROWS, :] * early[1:2, :]
     for n in range(MODES):
         response = response + read[n] * state[n : n + 1, :]
     out[...] = (query[...] * response).astype(out.dtype)
 
-    for d in range(1, ctx):
-        @pl.when(c + d < ctx)
-        def _(d=d):
-            pay_copy(d).wait_send()
+    to_later(lambda d: rim_copy(d).wait_send())
+    to_later(lambda d: pay_copy(d).wait_send())
+
+    @pl.when(c + 1 < ctx)
+    def _():
+        query_copy().wait_send()
+
     sent = buf.at[pl.ds(0, count - 1)]
     pltpu.make_async_copy(sent, sent, send_sem.at[0]).wait()
 
@@ -290,7 +322,7 @@
     count = lax.axis_size("tp")
     ctx = lax.axis_size("ctx")
     assert count == WIDE * DEEP
-    weight = jnp.transpose(in_weight, (1, 0, 2))
+    operands = (tokens, jnp.transpose(in_weight, (1, 0, 2)), filter_taps, decay_rate, residue)
     hbm = pl.BlockSpec(memory_space=pltpu.MemorySpace.HBM)
     f32 = jnp.float32
     scratch = [
@@ -309,14 +341,18 @@
         pltpu.VMEM((8, ROWS, LANES), f32),
         pltpu.VMEM((ROWS, LANES), f32),
         pltpu.VMEM((ROWS, LANES), f32),
-        pltpu.VMEM((32, LANES), f32),
-        pltpu.VMEM((ctx - 1, 32, LANES), f32),
+        pltpu.VMEM((MODES, LANES), f32),
+        pltpu.VMEM((ctx - 1, MODES, LANES), f32),
+        pltpu.VMEM((8, LANES), jnp.bfloat16),
+        pltpu.VMEM((ctx - 1, 8, LANES), jnp.bfloat16),
+        pltpu.VMEM((8, LANES), jnp.bfloat16),
+        pltpu.VMEM((8, LANES), jnp.bfloat16),
         pltpu.SemaphoreType.DMA((4,)),
         pltpu.SemaphoreType.DMA((count // GROUP,)),
         pltpu.SemaphoreType.DMA((1,)),
         pltpu.SemaphoreType.DMA((recv_count(),)),
-        pltpu.SemaphoreType.DMA((ctx - 1,)),
-        pltpu.SemaphoreType.DMA((ctx - 1,)),
+        pltpu.SemaphoreType.DMA((2 * ctx - 1,)),
+        pltpu.SemaphoreType.DMA((2 * ctx - 1,)),
     ]
 
     def kernel(*refs):
@@ -329,10 +365,10 @@
         out_specs=pl.BlockSpec(memory_space=pltpu.MemorySpace.VMEM),
         scratch_shapes=scratch,
         compiler_params=pltpu.CompilerParams(
-            collective_id=0, has_side_effects=True, vmem_limit_bytes=56 * 1024 * 1024
+            collective_id=0, has_side_effects=True, vmem_limit_bytes=48 * 1024 * 1024
         ),
         name="hyena",
-    )(tokens, weight, filter_taps, decay_rate, residue)
+    )(*(pltpu.with_memory_space_constraint(a, pltpu.MemorySpace.HBM) for a in operands))
 
 
 def solution(mesh):

time: 33.8 us -> 32.1 us (0.950)
  local copies, waits for them, and re-layouts: 1.47 us -> 0.63 us
  Pallas kernels: 32.2 us -> 31.4 us
    unnamed x1, local copies, waits for them, and re-layouts: 1.47 us -> 0.63 us
    pallas_call x1, Pallas kernels: 32.2 us -> 31.4 us  [on_device(): pl.pallas_call(kernel, out_shape=jax.ShapeDtypeStruct((ROWS, LANES), jnp....]
where the time goes in v3:
time: 32.1 us; the launch traced here: 32 us
  Pallas kernels  31.4 us (98%)
  local copies, waits for them, and re-layouts  0.63 us (2%)
    pallas_call x1, Pallas kernels, on_device(): pl.pallas_call(kernel, out_shape=jax.ShapeDtypeStruct((ROWS, LANES), jnp....  31.4 us

profile of v3, /device:TPU:5, one launch (start us, length us, event | category | flops | bytes accessed | tf_op | source)
XLA Modules:
  0.0 32.0 jit_solution(15807756542424387498)
XLA Ops:
  0.0 31.4 %hyena.1 = bf16[128,256]{1,0:T(8,128)(2,1)S(1)} custom-call(bf16[128,256]{1,0:T(8,128)(2,1)} %refs_0_.1, bf16[3,8192,256]{2,1,0:T(8,128)(2,1)} %bitcast.1, f32[3,3,256]{2,1,0:T(4,128)} %refs_2_.1, f32[16,256]{1,0:T(8,128)} %refs_3_.1, f32[16,256]{1,0:T(8,128)} %refs_4_.1), custom_call_target="tpu_custom_call" | custom-call | tf_op jit(solution)/shard_map/hyena/pallas_call | solution.py:361
  31.4 0.6 %copy.7 = bf16[128,256]{1,0:T(8,128)(2,1)} copy(bf16[128,256]{1,0:T(8,128)(2,1)S(1)} %hyena.1) | data formatting | bytes 131072

commit v4 on v3

--- a/solution.py
+++ b/solution.py
@@ -8,21 +8,21 @@
 MESH = pl.DeviceIdType.MESH
 PIECES = 2
 PLAN = (
-    (1, 0, 0, 1, 0), (0, 0, 0, 0, -1), (0, 0, 0, 0, 1), (0, 0, 0, -1, 0), (0, 0), (1, 0, 0, -1, 0), (1, 0, 0, 0, 1),
-    (1, 0, 0, 0, -1), (0, 0, 0, 1, 0), (1, 0, 0, 0, -2), (0, 0, 0, 0, 2), (0, 3, 0, 0, -1), (0, 0, 1, -1, 0),
-    (0, 0, 7, 1, 0), (1, 1, 0, 0, 1), (0, 0, 7, 0, -1), (1, 0, 7, 1, 0), (1, 0, 7, -1, 0), (1, 3, 0, 0, 1), (0, 1),
-    (0, 7), (1, 0), (3, 0), (0, 1, 0, 0, 1), (0, 1, 0, 1, 0), (1, 3, 0, -1, 0), (1, 0, 6, 0, -1), (1, 0, 6, -1, 0),
-    (0, 0, 2, 0, 1), (1, 0, 6, 1, 0), (1, 0, 6, 0, -2), (0, 0, 2, 1, 0), (0, 0, 2, -1, 0), (1, 1, 1, 0, 1),
-    (1, 1, 1, 1, 0), (0, 3, 7, -1, 0), (1, 3, 1, 0, 1), (0, 0, 6, 0, -1), (1, 3, 7, -1, 0), (0, 0, 6, 1, 0), (0, 6),
-    (1, 7), (3, 1), (3, 7), (0, 3, 7, 0, -1), (0, 2, 0, 0, 1), (1, 1), (2, 0), (1, 0, 5, -1, 0), (1, 0, 5, 1, 0),
-    (0, 0, 3, 0, 1), (0, 0, 3, -1, 0), (1, 3, 6, 0, -2), (0, 0, 3, 1, 0), (0, 1, 2, 0, 2), (0, 3, 2, -1, 0),
-    (1, 1, 2, 1, 0), (1, 2), (1, 0, 4, 1, 0), (0, 2, 7, 0, -1), (1, 3, 2, 0, 1), (3, 2), (0, 0, 5, -1, 0), (0, 5),
-    (0, 0, 5, 1, 0), (1, 2, 7, 0, -1), (1, 6), (2, 7), (1, 1, 2, 0, 1), (1, 0, 4, 0, -1), (2, 1), (3, 6),
-    (1, 3, 2, 1, 0), (1, 3, 5, -1, 0), (0, 2, 7, 0, -2), (0, 4), (0, 3, 3, 0, 1), (0, 3, 3, -1, 0), (1, 3, 4, -1, 0),
-    (0, 1, 4, 1, 0), (1, 2, 2, 0, 1), (2, 2), (1, 4), (3, 5), (3, 3), (2, 6), (1, 5), (1, 3), (0, 3), (0, 2), (3, 4),
-    (2, 5), (2, 3), (2, 4),
+    (1, 0, 0, -1, 0), (1, 0, 0, 0, 1), (0, 0, 0, 0, -1), (0, 0), (1, 0, 0, 0, -1), (1, 0, 0, 1, 0), (0, 0, 0, 0, 1),
+    (0, 0, 0, 0, 2), (0, 0, 0, 1, 0), (1, 0, 0, 0, -2), (0, 0, 0, -1, 0), (1, 0, 1, -1, 0), (0, 0, 7, 1, 0),
+    (1, 3, 0, 0, -1), (1, 0, 1, 0, 1), (0, 3, 0, 0, 1), (1, 0, 7, 1, 0), (0, 3, 0, -1, 0), (0, 3, 0, 0, -1), (0, 1),
+    (0, 7), (1, 0), (3, 0), (1, 1, 0, 0, 1), (0, 0, 1, 1, 0), (0, 0, 7, 0, -1), (1, 3, 0, -1, 0), (1, 0, 6, 0, -1),
+    (1, 0, 6, 1, 0), (0, 0, 2, -1, 0), (0, 0, 2, 0, 1), (1, 0, 6, -1, 0), (0, 0, 2, 1, 0), (0, 0, 2, 0, 2),
+    (1, 0, 6, 0, -2), (1, 0, 2, -1, 0), (0, 1, 7, 1, 0), (0, 2), (1, 0, 2, 0, 1), (1, 0, 2, 1, 0), (0, 1, 7, 0, -1),
+    (0, 3, 1, -1, 0), (1, 7), (3, 1), (3, 7), (1, 1, 7, 1, 0), (0, 0, 6, 0, -1), (1, 2, 0, 0, 1), (0, 0, 6, -1, 0),
+    (1, 1), (2, 0), (0, 3, 2, 0, 1), (1, 0, 5, 1, 0), (1, 0, 5, -1, 0), (1, 1, 6, 0, -2), (0, 6), (0, 1, 2, 0, 1),
+    (0, 0, 4, 1, 0), (0, 0, 4, -1, 0), (0, 4), (1, 0, 4, -1, 0), (0, 1, 2, 1, 0), (1, 3, 2, 0, 1), (0, 2, 7, 0, -1),
+    (1, 1, 6, 1, 0), (1, 3, 2, -1, 0), (1, 1, 2, 0, 1), (3, 2), (0, 1, 6, 0, -1), (0, 3), (1, 2), (1, 6),
+    (0, 3, 6, 0, -1), (1, 2, 1, 0, 2), (0, 5), (2, 1), (2, 7), (3, 6), (0, 2, 7, 0, -2), (1, 1, 5, 1, 0),
+    (0, 3, 3, -1, 0), (1, 1, 4, 1, 0), (0, 3, 4, -1, 0), (1, 4), (3, 3), (3, 4), (1, 3), (1, 5), (2, 2), (2, 6),
+    (3, 5), (2, 3), (2, 4), (2, 5),
 )
-AHEAD = 12
+AHEAD = 16
 FIRST_TABLE = 2
 LANES = 256
 ROWS = 128
@@ -90,6 +90,7 @@
     proj[:, 0:HALO, :] = jnp.zeros((3, HALO, LANES), jnp.float32)
     source[0:HALO, :] = jnp.zeros((HALO, LANES), jnp.float32)
     kern[...] = jnp.zeros_like(kern)
+    own.wait()
     pl.semaphore_wait(barrier, len(steps) + ctx - 1 - c)
 
     passed = {(h, (y, z)) for h, y, z, _, _ in sends}
@@ -102,9 +103,8 @@
 
     def piece_copy(step, h, v, w):
         rows = pl.ds(h * piece, piece)
-        src = tokens.at[rows] if v == (0, 0) else buf.at[slot(v), rows]
         return pltpu.make_async_remote_copy(
-            src_ref=src,
+            src_ref=buf.at[slot(v), rows],
             dst_ref=buf.at[slot(w), rows],
             send_sem=send_sem.at[0],
             recv_sem=recv_at(h, w),
@@ -145,8 +145,6 @@
                 kern_rows[r, q] = jnp.broadcast_to(rows[r : r + 1, :], (8, LANES))
 
     def multiply(order, v):
-        if v == (0, 0):
-            own.wait()
         for h in range(PIECES):
             if (h, v) in passed:
                 await_piece(h, v)

time: 32.1 us -> 31.9 us (level)
  no operation moved by 1% of the time
where the time goes in v4:
time: 31.9 us
  Pallas kernels  31.2 us (98%)
  local copies, waits for them, and re-layouts  0.63 us (2%)
    pallas_call x1, Pallas kernels, on_device(): pl.pallas_call(kernel, out_shape=jax.ShapeDtypeStruct((ROWS, LANES), jnp....  31.2 us

profile of v4, /device:TPU:5, one launch (start us, length us, event | category | flops | bytes accessed | tf_op | source)
XLA Modules:
  0.0 31.9 jit_solution(13258230665259979911)
XLA Ops:
  0.0 31.2 %hyena.1 = bf16[128,256]{1,0:T(8,128)(2,1)S(1)} custom-call(bf16[128,256]{1,0:T(8,128)(2,1)} %refs_0_.1, bf16[3,8192,256]{2,1,0:T(8,128)(2,1)} %bitcast.1, f32[3,3,256]{2,1,0:T(4,128)} %refs_2_.1, f32[16,256]{1,0:T(8,128)} %refs_3_.1, f32[16,256]{1,0:T(8,128)} %refs_4_.1), custom_call_target="tpu_custom_call" | custom-call | tf_op jit(solution)/shard_map/hyena/pallas_call | solution.py:359
  31.2 0.6 %copy.7 = bf16[128,256]{1,0:T(8,128)(2,1)} copy(bf16[128,256]{1,0:T(8,128)(2,1)S(1)} %hyena.1) | data formatting | bytes 131072

commit v5 on v4

--- a/solution.py
+++ b/solution.py
@@ -144,17 +144,20 @@
             for r in range(8):
                 kern_rows[r, q] = jnp.broadcast_to(rows[r : r + 1, :], (8, LANES))
 
-    def multiply(order, v):
-        for h in range(PIECES):
-            if (h, v) in passed:
-                await_piece(h, v)
-        await_leaves(v)
-        if order % GROUP == 0:
-            weight_wait(order // GROUP)
-        lhs = buf[slot(v)]
+    def multiply(order):
+        pair = blocks[order - 1 : order + 1]
+        for v in pair:
+            for h in range(PIECES):
+                if (h, v) in passed:
+                    await_piece(h, v)
+            await_leaves(v)
+        if (order - 1) % GROUP == 0:
+            weight_wait((order - 1) // GROUP)
         for s in range(3):
-            part = jnp.dot(lhs, wbuf[slot(v), s], preferred_element_type=jnp.float32)
-            if order == 0:
+            part = sum(
+                jnp.dot(buf[slot(v)], wbuf[slot(v), s], preferred_element_type=jnp.float32) for v in pair
+            )
+            if order == 1:
                 acc[s] = part
             else:
                 acc[s] += part
@@ -170,7 +173,8 @@
         i = slot(p)
         if i + AHEAD < count:
             weight_copy(blocks[i + AHEAD]).start()
-        multiply(i, p)
+        if i % 2 == 1:
+            multiply(i)
         if tables < MODES and i >= FIRST_TABLE:
             table(tables)
             tables += 1

time: 31.9 us -> 31.6 us (level)
  no operation moved by 1% of the time
where the time goes in v5:
time: 31.6 us
  Pallas kernels  30.9 us (98%)
  local copies, waits for them, and re-layouts  0.63 us (2%)
    pallas_call x1, Pallas kernels, on_device(): pl.pallas_call(kernel, out_shape=jax.ShapeDtypeStruct((ROWS, LANES), jnp....  30.9 us
    unnamed x1, local copies, waits for them, and re-layouts  0.63 us

profile of v5, /device:TPU:5, one launch (start us, length us, event | category | flops | bytes accessed | tf_op | source)
XLA Modules:
  0.0 31.6 jit_solution(3831082365413311152)
XLA Ops:
  0.0 30.9 %hyena.1 = bf16[128,256]{1,0:T(8,128)(2,1)S(1)} custom-call(bf16[128,256]{1,0:T(8,128)(2,1)} %refs_0_.1, bf16[3,8192,256]{2,1,0:T(8,128)(2,1)} %bitcast.1, f32[3,3,256]{2,1,0:T(4,128)} %refs_2_.1, f32[16,256]{1,0:T(8,128)} %refs_3_.1, f32[16,256]{1,0:T(8,128)} %refs_4_.1), custom_call_target="tpu_custom_call" | custom-call | tf_op jit(solution)/shard_map/hyena/pallas_call | solution.py:363
  30.9 0.6 %copy.7 = bf16[128,256]{1,0:T(8,128)(2,1)} copy(bf16[128,256]{1,0:T(8,128)(2,1)S(1)} %hyena.1) | data formatting | bytes 131072

commit v6 on v5

--- a/solution.py
+++ b/solution.py
@@ -98,8 +98,10 @@
     order_of = {p: i for i, p in enumerate(kept)}
     leaves = {v: [h for h in range(PIECES) if (h, v) not in passed] for v in blocks}
 
+    leafy = [v for v in blocks if leaves[v] and v != (0, 0)]
+
     def recv_at(h, w):
-        return recv_sem.at[order_of[h, w] if (h, w) in passed else len(kept) + slot(w)]
+        return recv_sem.at[order_of[h, w] if (h, w) in passed else len(kept) + leafy.index(w)]
 
     def piece_copy(step, h, v, w):
         rows = pl.ds(h * piece, piece)
@@ -316,8 +318,10 @@
 
 
 def recv_count():
-    passed = {p[:3] for p in PLAN if len(p) == 5 and p[1:3] != (0, 0)}
-    return len(passed) + WIDE * DEEP
+    passed = {p[:3] for p in PLAN if len(p) == 5}
+    blocks = [p for p in PLAN if len(p) == 2 and p != (0, 0)]
+    kept = sum(p[1:] != (0, 0) for p in passed)
+    return kept + sum(any((h, *v) not in passed for h in range(PIECES)) for v in blocks)
 
 
 def on_device(tokens, in_weight, filter_taps, decay_rate, residue):

time: 31.6 us -> 31.5 us (level)
  no operation moved by 1% of the time
where the time goes in v6:
time: 31.5 us
  Pallas kernels  30.8 us (98%)
  local copies, waits for them, and re-layouts  0.63 us (2%)
    pallas_call x1, Pallas kernels, on_device(): pl.pallas_call(kernel, out_shape=jax.ShapeDtypeStruct((ROWS, LANES), jnp....  30.8 us
    unnamed x1, local copies, waits for them, and re-layouts  0.63 us

profile of v6, /device:TPU:5, one launch (start us, length us, event | category | flops | bytes accessed | tf_op | source)
XLA Modules:
  0.0 31.5 jit_solution(465926021880968527)
XLA Ops:
  0.0 30.8 %hyena.1 = bf16[128,256]{1,0:T(8,128)(2,1)S(1)} custom-call(bf16[128,256]{1,0:T(8,128)(2,1)} %refs_0_.1, bf16[3,8192,256]{2,1,0:T(8,128)(2,1)} %bitcast.1, f32[3,3,256]{2,1,0:T(4,128)} %refs_2_.1, f32[16,256]{1,0:T(8,128)} %refs_3_.1, f32[16,256]{1,0:T(8,128)} %refs_4_.1), custom_call_target="tpu_custom_call" | custom-call | tf_op jit(solution)/shard_map/hyena/pallas_call | solution.py:367
  30.8 0.6 %copy.7 = bf16[128,256]{1,0:T(8,128)(2,1)} copy(bf16[128,256]{1,0:T(8,128)(2,1)S(1)} %hyena.1) | data formatting | bytes 131072
